TPU v7x, 128 devices: a whole 4x4x4 slice. The times are simulated.
128 devices in a mesh: ublk: 16 (over x, z), salt: 8 (over y, core).
Axes of the slice: x: 4, y: 4, z: 4, core: 2. Of those that a mesh axis runs over, the one named last changes fastest.
Arguments:
- user_factors: bfloat16 [16, 8192, 256], P('ublk', 'salt')
- tile_users: int32 [16, 8, 4096], P('ublk', 'salt'), may hold values from 0 to 8191
- tile_items: int32 [16, 8, 4096], P('ublk', 'salt'), may hold values from 0 to 511
- tile_weight: float32 [16, 8, 4096], P('ublk', 'salt'), may hold values from 0.5 to 8
- live_count: int32 [16, 8], P('ublk', 'salt'), may hold values from 2048 to 4096, as said below
Outputs:
- item_factors: float32 [8, 512, 256], P('salt', 'ublk')
- residual: float32 [8, 512, 256], P('salt', 'ublk')
Inputs may be any that keep to these rules, and one draw needn't show every extreme that they name: Every entry of live_count is at least 2048 and at most 4096; some tile is full.
All inputs are finite; a program needn't handle non-finite values.
Results may differ from a plain program's by a relative error of at most 0.0022.
Values may be sent and summed in bfloat16 or wider, within the bound.
A program may use at most 64 MiB of HBM per device.

v0:
```python
import jax
import jax.numpy as jnp
from jax import lax
from jax.sharding import PartitionSpec as P

ITERS = 8
ITEM_DEV = 32
REG = 1.0
EPS = 1e-06


def conjugate(rhs, image_of):
    solution = jnp.zeros_like(rhs)
    resid = rhs
    direction = rhs
    norm_now = jnp.sum(resid * resid, axis=1)
    for step in range(ITERS):
        image = image_of(direction)
        alpha = norm_now / (jnp.sum(direction * image, axis=1) + EPS)
        solution = solution + alpha[:, None] * direction
        resid = resid - alpha[:, None] * image
        norm_next = jnp.sum(resid * resid, axis=1)
        direction = resid + (norm_next / (norm_now + EPS))[:, None] * direction
        norm_now = norm_next
    return (solution, resid)


def body(user_factors, tile_users, tile_items, tile_weight, live_count):
    shard = user_factors[0]
    block = lax.all_gather(shard, "salt", axis=0, tiled=True)
    contract = (((0,), (0,)), ((), ()))
    own_gram = lax.dot_general(shard, shard, contract, preferred_element_type=jnp.float32)
    gram = lax.psum(own_gram, ("ublk", "salt"))
    users = tile_users[0, 0]
    items = tile_items[0, 0]
    raw = tile_weight[0, 0]
    live = jnp.arange(users.shape[0], dtype=jnp.int32) < live_count[0, 0]
    weight = jnp.where(live, raw, jnp.zeros_like(raw))
    confid = jnp.where(live, 1.0 + raw, jnp.zeros_like(raw))
    rows = jnp.take(block, users, axis=0).astype(jnp.float32)
    column_items = ITEM_DEV * lax.axis_size("ublk")
    rhs_terms = jax.ops.segment_sum(confid[:, None] * rows, items, num_segments=column_items)

    def local_terms(whole_dir):
        along = jnp.sum(rows * whole_dir[items], axis=1) * weight
        return jax.ops.segment_sum(along[:, None] * rows, items, num_segments=column_items)

    def finish(summed, direction):
        return summed + jnp.dot(direction, gram, precision=lax.Precision.HIGHEST) + REG * direction

    rhs = lax.psum(rhs_terms, "ublk")

    def image_every(direction):
        summed = lax.psum(local_terms(direction), "ublk")
        return finish(summed, direction)

    solution_all, resid_all = conjugate(rhs, image_every)
    start = lax.axis_index("ublk") * ITEM_DEV
    solution = lax.dynamic_slice_in_dim(solution_all, start, ITEM_DEV, 0)
    resid = lax.dynamic_slice_in_dim(resid_all, start, ITEM_DEV, 0)
    return (solution[None], resid[None])


def solution(mesh):
    return jax.shard_map(
        body,
        mesh=mesh,
        in_specs=(
            P("ublk", "salt", None),
            P("ublk", "salt", None),
            P("ublk", "salt", None),
            P("ublk", "salt", None),
            P("ublk", "salt"),
        ),
        out_specs=(P("salt", "ublk", None), P("salt", "ublk", None)),
        check_vma=False,
    )
```

profile of v0, /device:TPU:0, one launch (start us, length us, event | category | flops | bytes accessed | tf_op | source)
XLA Modules:
  0.0 1352.9 jit_solution(7503660293953594438)
XLA Ops:
  10.8 33.5 %all-gather.3.cloned.1.call-done = bf16[1,8192,256]{2,1,0:T(8,128)(2,1)} async-done(((bf16[1,1024,256]{2,1,0:T(8,128)(2,1)}), bf16[1,8192,256]{2,1,0:T(8,128)(2,1)}) %all-gather.3.cloned.1.call-update) | async-done | bytes 4194320 | tf_op jit(solution)/shard_map/all_gather | solution.py:30
  44.3 15.8 %gather_fusion = bf16[4096,256]{1,0:T(8,128)(2,1)S(1)} fusion(bf16[8192,256]{1,0:T(8,128)(2,1)} %bitcast.43, s32[4096]{0:T(1024)S(1)} %broadcast_clamp_fusion.1), kind=kCustom, calls=%fused_computation | custom fusion | bytes 4210688 | tf_op jit(solution)/shard_map/jit(_take)/gather | solution.py:40
  60.1 26.1 %scatter_custom_fusion = f32[512,256]{1,0:T(8,128)} fusion(s32[4096]{0:T(1024)S(1)} %bitcast.56, f32[4096]{0:T(1024)S(1)} %add_select_fusion, f32[]{:T(128)} %constant.11.clone.1, bf16[4096,256]{1,0:T(8,128)(2,1)S(1)} %gather_fusion, pred[4096]{0:T(1024)(128)(4,1)S(1)} %compare_and_fusion), kind=kCustom, calls=%fused_computation.35 | custom fusion | flops 4194304 | bytes 2641924 | tf_op jit(solution)/shard_map/scatter-add | solution.py:42
  87.4 84.7 %all-reduce.11.cloned.1.call-done = f32[512,256]{1,0:T(8,128)} async-done(((f32[512,256]{1,0:T(8,128)}), f32[512,256]{1,0:T(8,128)}) %all-reduce.11.cloned.1.call-update) | async-done | bytes 524304 | tf_op jit(solution)/shard_map/psum | solution.py:51
  172.1 17.1 %gather_fusion.1 = f32[4096,256]{1,0:T(8,128)} fusion(f32[512,256]{1,0:T(8,128)} %all-reduce.11.cloned.1.call-done, s32[4096]{0:T(1024)S(1)} %broadcast_clamp_fusion), kind=kCustom, calls=%fused_computation.1 | custom fusion | bytes 8404992 | tf_op jit(solution)/shard_map/gather | solution.py:45
  189.2 3.0 fusion.1
  192.2 26.1 %scatter_custom_fusion.1 = f32[512,256]{1,0:T(8,128)} fusion(s32[4096]{0:T(1024)S(1)} %bitcast.57, f32[4096]{0:T(1024)S(1)} %fusion.60, f32[]{:T(128)} %constant.11.clone.1, bf16[4096,256]{1,0:T(8,128)(2,1)S(1)} %gather_fusion, pred[4096]{0:T(1024)(128)(4,1)S(1)} %compare_and_fusion), kind=kCustom, calls=%fused_computation.37 | custom fusion | flops 4194304 | bytes 2641924 | tf_op jit(solution)/shard_map/scatter-add | solution.py:46
  218.7 100.7 %all-reduce.15.cloned.1.call-done = f32[256,256]{1,0:T(8,128)} async-done(((f32[256,256]{1,0:T(8,128)}), f32[256,256]{1,0:T(8,128)}) %all-reduce.15.cloned.1.call-update) | async-done | bytes 262160 | tf_op jit(solution)/shard_map/psum | solution.py:33
  319.4 86.2 %all-reduce.13.cloned.1.call-done = f32[512,256]{1,0:T(8,128)} async-done(((f32[512,256]{1,0:T(8,128)}), f32[512,256]{1,0:T(8,128)}) %all-reduce.13.cloned.1.call-update) | async-done | bytes 524304 | tf_op jit(solution)/shard_map/psum | solution.py:54
  405.6 1.8 multiply_reduce_fusion.14
  408.4 16.1 %gather_fusion.2 = f32[4096,256]{1,0:T(8,128)} fusion(f32[512,256]{1,0:T(8,128)S(1)} %multiply_add_fusion.7, s32[4096]{0:T(1024)S(1)} %broadcast_clamp_fusion), kind=kCustom, calls=%fused_computation.2 | custom fusion | bytes 8404992 | tf_op jit(solution)/shard_map/gather | solution.py:45
  424.5 3.0 fusion.3
  427.5 26.1 %scatter_custom_fusion.2 = f32[512,256]{1,0:T(8,128)} fusion(s32[4096]{0:T(1024)S(1)} %bitcast.58, f32[4096]{0:T(1024)S(1)} %fusion.59, f32[]{:T(128)} %constant.11.clone.1, bf16[4096,256]{1,0:T(8,128)(2,1)S(1)} %gather_fusion, pred[4096]{0:T(1024)(128)(4,1)S(1)} %compare_and_fusion), kind=kCustom, calls=%fused_computation.39 | custom fusion | flops 4194304 | bytes 2641924 | tf_op jit(solution)/shard_map/scatter-add | solution.py:46
  453.7 85.3 %all-reduce.17.cloned.1.call-done = f32[512,256]{1,0:T(8,128)} async-done(((f32[512,256]{1,0:T(8,128)}), f32[512,256]{1,0:T(8,128)}) %all-reduce.17.cloned.1.call-update) | async-done | bytes 524304 | tf_op jit(solution)/shard_map/psum | solution.py:54
  539.0 1.7 multiply_reduce_fusion.12
  540.7 2.1 multiply_reduce_fusion.11
  542.9 16.1 %gather_fusion.3 = f32[4096,256]{1,0:T(8,128)} fusion(f32[512,256]{1,0:T(8,128)S(1)} %multiply_add_fusion.5, s32[4096]{0:T(1024)S(1)} %broadcast_clamp_fusion), kind=kCustom, calls=%fused_computation.3 | custom fusion | bytes 8404992 | tf_op jit(solution)/shard_map/gather | solution.py:45
  559.0 3.5 fusion.5
  562.5 26.5 %scatter_custom_fusion.3 = f32[512,256]{1,0:T(8,128)} fusion(s32[4096]{0:T(1024)S(1)} %bitcast.59, f32[4096]{0:T(1024)S(1)} %fusion.58, f32[]{:T(128)} %constant.11.clone.1, bf16[4096,256]{1,0:T(8,128)(2,1)} %copy-done.1, pred[4096]{0:T(1024)(128)(4,1)S(1)} %compare_and_fusion), kind=kCustom, calls=%fused_computation.41 | custom fusion | flops 4194304 | bytes 2641924 | tf_op jit(solution)/shard_map/scatter-add | solution.py:46
  589.6 84.6 %all-reduce.19.cloned.1.call-done = f32[512,256]{1,0:T(8,128)} async-done(((f32[512,256]{1,0:T(8,128)}), f32[512,256]{1,0:T(8,128)}) %all-reduce.19.cloned.1.call-update) | async-done | bytes 524304 | tf_op jit(solution)/shard_map/psum | solution.py:54
  674.3 1.7 multiply_reduce_fusion.10
  677.3 16.1 %gather_fusion.4 = f32[4096,256]{1,0:T(8,128)} fusion(f32[512,256]{1,0:T(8,128)S(1)} %get-tuple-element.18, s32[4096]{0:T(1024)S(1)} %broadcast_clamp_fusion), kind=kCustom, calls=%fused_computation.4 | custom fusion | bytes 8404992 | tf_op jit(solution)/shard_map/gather | solution.py:45
  693.3 3.0 fusion.7
  696.4 26.1 %scatter_custom_fusion.4 = f32[512,256]{1,0:T(8,128)} fusion(s32[4096]{0:T(1024)S(1)} %bitcast.60, f32[4096]{0:T(1024)S(1)} %fusion.57, f32[]{:T(128)} %constant.11.clone.1, bf16[4096,256]{1,0:T(8,128)(2,1)S(1)} %copy-done.2, pred[4096]{0:T(1024)(128)(4,1)S(1)} %compare_and_fusion), kind=kCustom, calls=%fused_computation.43 | custom fusion | flops 4194304 | bytes 2641924 | tf_op jit(solution)/shard_map/scatter-add | solution.py:46
  722.6 85.2 %all-reduce.21.cloned.1.call-done = f32[512,256]{1,0:T(8,128)} async-done(((f32[512,256]{1,0:T(8,128)}), f32[512,256]{1,0:T(8,128)}) %all-reduce.21.cloned.1.call-update) | async-done | bytes 524304 | tf_op jit(solution)/shard_map/psum | solution.py:54
  807.8 1.7 multiply_reduce_fusion.8
  810.7 16.1 %gather_fusion.5 = f32[4096,256]{1,0:T(8,128)} fusion(f32[512,256]{1,0:T(8,128)S(1)} %multiply_add_fusion.3, s32[4096]{0:T(1024)S(1)} %broadcast_clamp_fusion), kind=kCustom, calls=%fused_computation.5 | custom fusion | bytes 8404992 | tf_op jit(solution)/shard_map/gather | solution.py:45
  826.8 2.9 fusion.9
  829.7 26.1 %scatter_custom_fusion.5 = f32[512,256]{1,0:T(8,128)} fusion(s32[4096]{0:T(1024)S(1)} %bitcast.61, f32[4096]{0:T(1024)S(1)} %fusion.56, f32[]{:T(128)} %constant.11.clone.1, bf16[4096,256]{1,0:T(8,128)(2,1)S(1)} %copy-done.2, pred[4096]{0:T(1024)(128)(4,1)S(1)} %compare_and_fusion), kind=kCustom, calls=%fused_computation.45 | custom fusion | flops 4194304 | bytes 2641924 | tf_op jit(solution)/shard_map/scatter-add | solution.py:46
  856.1 85.1 %all-reduce.23.cloned.1.call-done = f32[512,256]{1,0:T(8,128)} async-done(((f32[512,256]{1,0:T(8,128)}), f32[512,256]{1,0:T(8,128)}) %all-reduce.23.cloned.1.call-update) | async-done | bytes 524304 | tf_op jit(solution)/shard_map/psum | solution.py:54
  941.2 1.7 multiply_reduce_fusion.6
  942.9 1.3 multiply_reduce_fusion.5
  944.4 16.1 %gather_fusion.6 = f32[4096,256]{1,0:T(8,128)} fusion(f32[512,256]{1,0:T(8,128)S(1)} %multiply_add_fusion.2, s32[4096]{0:T(1024)S(1)} %broadcast_clamp_fusion), kind=kCustom, calls=%fused_computation.6 | custom fusion | bytes 8404992 | tf_op jit(solution)/shard_map/gather | solution.py:45
  960.4 3.5 fusion.11
  963.9 26.5 %scatter_custom_fusion.6 = f32[512,256]{1,0:T(8,128)} fusion(s32[4096]{0:T(1024)S(1)} %bitcast.62, f32[4096]{0:T(1024)S(1)} %fusion.55, f32[]{:T(128)} %constant.11.clone.1, bf16[4096,256]{1,0:T(8,128)(2,1)} %copy-done.1, pred[4096]{0:T(1024)(128)(4,1)S(1)} %compare_and_fusion), kind=kCustom, calls=%fused_computation.47 | custom fusion | flops 4194304 | bytes 2641924 | tf_op jit(solution)/shard_map/scatter-add | solution.py:46
  990.5 85.2 %all-reduce.25.cloned.1.call-done = f32[512,256]{1,0:T(8,128)} async-done(((f32[512,256]{1,0:T(8,128)}), f32[512,256]{1,0:T(8,128)}) %all-reduce.25.cloned.1.call-update) | async-done | bytes 524304 | tf_op jit(solution)/shard_map/psum | solution.py:54
  1075.8 1.7 multiply_reduce_fusion.4
  1077.9 16.1 %gather_fusion.7 = f32[4096,256]{1,0:T(8,128)} fusion(f32[512,256]{1,0:T(8,128)S(1)} %multiply_add_fusion.1, s32[4096]{0:T(1024)S(1)} %broadcast_clamp_fusion), kind=kCustom, calls=%fused_computation.7 | custom fusion | bytes 8404992 | tf_op jit(solution)/shard_map/gather | solution.py:45
  1094.0 3.5 fusion.13
  1097.5 26.5 %scatter_custom_fusion.7 = f32[512,256]{1,0:T(8,128)} fusion(s32[4096]{0:T(1024)S(1)} %bitcast.63, f32[4096]{0:T(1024)S(1)} %fusion.54, f32[]{:T(128)} %constant.11.clone.1, bf16[4096,256]{1,0:T(8,128)(2,1)} %copy-done.1, pred[4096]{0:T(1024)(128)(4,1)S(1)} %compare_and_fusion), kind=kCustom, calls=%fused_computation.49 | custom fusion | flops 4194304 | bytes 2641924 | tf_op jit(solution)/shard_map/scatter-add | solution.py:46
  1124.3 85.0 %all-reduce.27.cloned.1.call-done = f32[512,256]{1,0:T(8,128)} async-done(((f32[512,256]{1,0:T(8,128)}), f32[512,256]{1,0:T(8,128)}) %all-reduce.27.cloned.1.call-update) | async-done | bytes 524304 | tf_op jit(solution)/shard_map/psum | solution.py:54
  1209.3 1.7 multiply_reduce_fusion.2
  1211.4 16.1 %gather_fusion.8 = f32[4096,256]{1,0:T(8,128)} fusion(f32[512,256]{1,0:T(8,128)S(1)} %multiply_add_fusion, s32[4096]{0:T(1024)S(1)} %broadcast_clamp_fusion), kind=kCustom, calls=%fused_computation.8 | custom fusion | bytes 8404992 | tf_op jit(solution)/shard_map/gather | solution.py:45
  1227.5 3.5 fusion.15
  1231.0 26.5 %scatter_custom_fusion.8 = f32[512,256]{1,0:T(8,128)} fusion(s32[4096]{0:T(1024)S(1)} %bitcast.64, f32[4096]{0:T(1024)S(1)} %fusion.53, f32[]{:T(128)} %constant.11.clone.1, bf16[4096,256]{1,0:T(8,128)(2,1)} %copy-done.1, pred[4096]{0:T(1024)(128)(4,1)S(1)} %compare_and_fusion), kind=kCustom, calls=%fused_computation.51 | custom fusion | flops 4194304 | bytes 2641924 | tf_op jit(solution)/shard_map/scatter-add | solution.py:46
  1257.8 85.0 %all-reduce.29.cloned.1.call-done = f32[512,256]{1,0:T(8,128)} async-done(((f32[512,256]{1,0:T(8,128)}), f32[512,256]{1,0:T(8,128)}) %all-reduce.29.cloned.1.call-update) | async-done | bytes 524304 | tf_op jit(solution)/shard_map/psum | solution.py:54
  1342.8 1.7 multiply_reduce_fusion
  1344.6 1.5 fusion.45
  (91 shorter events, 10.8 us)
Async XLA Ops:
  7.2 37.1 %all-gather.3.cloned.1.call-start = ((), (), s32[]{:S(2)}) async-start(), calls=%async_computation.10 | async-start | bytes 4718592 | tf_op jit(solution)/shard_map/all_gather | solution.py:30
  7.9 164.2 %all-reduce.11.cloned.1.call-start = ((), (), s32[]{:S(2)}) async-start(), calls=%async_computation | async-start | bytes 1048576 | tf_op jit(solution)/shard_map/psum | solution.py:51
  44.3 15.8 %copy-start.10 = (s32[1,1,4096]{2,1,0:T(1,128)S(1)}, s32[1,1,4096]{2,1,0:T(1,128)}, u32[]{:S(2)}) copy-start(s32[1,1,4096]{2,1,0:T(1,128)} %param.7) | copy-start | bytes 49156
  44.3 42.0 %copy-start.9 = (bf16[1,1024,256]{2,1,0:T(8,128)(2,1)S(1)}, bf16[1,1024,256]{2,1,0:T(8,128)(2,1)}, u32[]{:S(2)}) copy-start(bf16[1,1024,256]{2,1,0:T(8,128)(2,1)} %param.5) | copy-start | bytes 1572868
  60.1 367.5 %copy-start.1 = (bf16[4096,256]{1,0:T(8,128)(2,1)}, bf16[4096,256]{1,0:T(8,128)(2,1)S(1)}, u32[]{:S(2)}) copy-start(bf16[4096,256]{1,0:T(8,128)(2,1)S(1)} %gather_fusion) | copy-start | bytes 6291460
  86.2 233.2 %all-reduce.15.cloned.1.call-start = ((), (), s32[]{:S(2)}) async-start(), calls=%async_computation.2 | async-start | bytes 524288 | tf_op jit(solution)/shard_map/psum | solution.py:33
  87.3 318.2 %all-reduce.13.cloned.1.call-start = ((), (), s32[]{:S(2)}) async-start(), calls=%async_computation.1 | async-start | bytes 1048576 | tf_op jit(solution)/shard_map/psum | solution.py:54
  189.2 3.0 copy-start.8
  189.2 216.4 %copy-start = (f32[512,256]{1,0:T(8,128)S(1)}, f32[512,256]{1,0:T(8,128)}, u32[]{:S(2)}) copy-start(f32[512,256]{1,0:T(8,128)} %all-reduce.11.cloned.1.call-done) | copy-start | bytes 1572868
  218.4 320.6 %all-reduce.17.cloned.1.call-start = ((), (), s32[]{:S(2)}) async-start(), calls=%async_computation.3 | async-start | bytes 1048576 | tf_op jit(solution)/shard_map/psum | solution.py:54
  407.4 0.8 copy-start.4
  424.5 114.5 %copy-start.3 = (f32[256,256]{1,0:T(8,128)S(1)}, f32[256,256]{1,0:T(8,128)}, u32[]{:S(2)}) copy-start(f32[256,256]{1,0:T(8,128)} %all-reduce.15.cloned.1.call-done) | copy-start | bytes 786436
  453.6 220.6 %all-reduce.19.cloned.1.call-start = ((), (), s32[]{:S(2)}) async-start(), calls=%async_computation.4 | async-start | bytes 1048576 | tf_op jit(solution)/shard_map/psum | solution.py:54
  589.0 218.8 %all-reduce.21.cloned.1.call-start = ((), (), s32[]{:S(2)}) async-start(), calls=%async_computation.5 | async-start | bytes 1048576 | tf_op jit(solution)/shard_map/psum | solution.py:54
  676.2 1.0 copy-start.6
  677.3 16.1 %copy-start.2 = (bf16[4096,256]{1,0:T(8,128)(2,1)S(1)}, bf16[4096,256]{1,0:T(8,128)(2,1)}, u32[]{:S(2)}) copy-start(bf16[4096,256]{1,0:T(8,128)(2,1)} %copy-done.1) | copy-start | bytes 6291460
  693.3 116.2 %copy-start.7 = (f32[512,256]{1,0:T(8,128)S(1)}, f32[512,256]{1,0:T(8,128)}, u32[]{:S(2)}) copy-start(f32[512,256]{1,0:T(8,128)} %copy-done.6) | copy-start | bytes 1572868
  722.5 218.7 %all-reduce.23.cloned.1.call-start = ((), (), s32[]{:S(2)}) async-start(), calls=%async_computation.6 | async-start | bytes 1048576 | tf_op jit(solution)/shard_map/psum | solution.py:54
  809.8 0.8 copy-start.5
  855.9 219.9 %all-reduce.25.cloned.1.call-start = ((), (), s32[]{:S(2)}) async-start(), calls=%async_computation.7 | async-start | bytes 1048576 | tf_op jit(solution)/shard_map/psum | solution.py:54
  990.5 218.8 %all-reduce.27.cloned.1.call-start = ((), (), s32[]{:S(2)}) async-start(), calls=%async_computation.8 | async-start | bytes 1048576 | tf_op jit(solution)/shard_map/psum | solution.py:54
  1124.0 218.8 %all-reduce.29.cloned.1.call-start = ((), (), s32[]{:S(2)}) async-start(), calls=%async_computation.9 | async-start | bytes 1048576 | tf_op jit(solution)/shard_map/psum | solution.py:54
Sparse Core Ops, SparseCore 0:
  9.7 34.5 all-gather.2
  86.3 85.7 all-reduce.10
  176.8 142.5 all-reduce.14
  322.5 83.0 all-reduce.12
  453.8 85.1 all-reduce.16
  589.2 85.0 all-reduce.18
  722.6 85.1 all-reduce.20
  856.0 85.1 all-reduce.22
  990.6 85.1 all-reduce.24
  1124.1 85.1 all-reduce.26
  1257.6 85.1 all-reduce.28
where the time goes:
time: 1360 us; the launch traced here: 1350 us
  waiting for transfers between devices  901 us (66%)
  other arithmetic  273 us (20%)
  local copies, waits for them, and re-layouts  147 us (11%)
  between operations  15.1 us (1%)
  matrix products  14.8 us (1%)
    psum x8, waiting for transfers between devices, image_every(): summed = lax.psum(local_terms(direction), 'ublk')  682 us
    scatter-add x8, other arithmetic, local_terms(): jax.ops.segment_sum(along[:, None] * rows, items, num_segments=column_items)  210 us
    gather x8, local copies, waits for them, and re-layouts, local_terms(): along = jnp.sum(rows * whole_dir[items], axis=1) * weight  130 us
    psum x1, waiting for transfers between devices, body(): gram = lax.psum(own_gram, ('ublk', 'salt'))  101 us
    psum x1, waiting for transfers between devices, body(): rhs = lax.psum(rhs_terms, 'ublk')  84.7 us
    all_gather x1, waiting for transfers between devices, body(): block = lax.all_gather(shard, 'salt', axis=0, tiled=True)  33.5 us
  transfers between devices with their start and end apart: 11, of which 11 were waited for; matrix products, arithmetic and copies ran while one was open for 4% of the time, Pallas kernels for 0%

commit v1 on v0

--- a/solution.py
+++ b/solution.py
@@ -30,7 +30,7 @@
     block = lax.all_gather(shard, "salt", axis=0, tiled=True)
     contract = (((0,), (0,)), ((), ()))
     own_gram = lax.dot_general(shard, shard, contract, preferred_element_type=jnp.float32)
-    gram = lax.psum(own_gram, ("ublk", "salt"))
+    gram = lax.psum(lax.psum(own_gram, "salt"), "ublk")
     users = tile_users[0, 0]
     items = tile_items[0, 0]
     raw = tile_weight[0, 0]

time: 1360 us -> 1280 us (0.941)
  waiting for transfers between devices: 901 us -> 819 us
    psum x1, waiting for transfers between devices: 101 us -> 15.8 us  [body(): gram = lax.psum(lax.psum(own_gram, 'salt'), 'ublk')]
where the time goes in v1:
time: 1280 us; the launch traced here: 1270 us
  waiting for transfers between devices  819 us (64%)
  other arithmetic  273 us (21%)
  local copies, waits for them, and re-layouts  147 us (11%)
  between operations  15.1 us (1%)
  matrix products  14.8 us (1%)
    psum x8, waiting for transfers between devices, image_every(): summed = lax.psum(local_terms(direction), 'ublk')  684 us
    scatter-add x8, other arithmetic, local_terms(): jax.ops.segment_sum(along[:, None] * rows, items, num_segments=column_items)  210 us
    gather x8, local copies, waits for them, and re-layouts, local_terms(): along = jnp.sum(rows * whole_dir[items], axis=1) * weight  130 us
    psum x1, waiting for transfers between devices, body(): rhs = lax.psum(rhs_terms, 'ublk')  84.7 us
    all_gather x1, waiting for transfers between devices, body(): block = lax.all_gather(shard, 'salt', axis=0, tiled=True)  33.5 us
    scatter-add x1, other arithmetic, body(): jax.ops.segment_sum(confid[:, None] * rows, items, num_segments=column_it...  26.1 us
    reduce_sum x8, other arithmetic, local_terms(): along = jnp.sum(rows * whole_dir[items], axis=1) * weight  25.8 us
  transfers between devices with their start and end apart: 11, of which 11 were waited for; matrix products, arithmetic and copies ran while one was open for 4% of the time, Pallas kernels for 0%

profile of v1, /device:TPU:0, one launch (start us, length us, event | category | flops | bytes accessed | tf_op | source)
XLA Modules:
  0.0 1270.4 jit_solution(4681333530305206388)
XLA Ops:
  10.8 33.5 %all-gather.3.cloned.1.call-done = bf16[1,8192,256]{2,1,0:T(8,128)(2,1)} async-done(((bf16[1,1024,256]{2,1,0:T(8,128)(2,1)}), bf16[1,8192,256]{2,1,0:T(8,128)(2,1)}) %all-gather.3.cloned.1.call-update) | async-done | bytes 4194320 | tf_op jit(solution)/shard_map/all_gather | solution.py:30
  44.3 15.8 %gather_fusion = bf16[4096,256]{1,0:T(8,128)(2,1)S(1)} fusion(bf16[8192,256]{1,0:T(8,128)(2,1)} %bitcast.43, s32[4096]{0:T(1024)S(1)} %broadcast_clamp_fusion.1), kind=kCustom, calls=%fused_computation | custom fusion | bytes 4210688 | tf_op jit(solution)/shard_map/jit(_take)/gather | solution.py:40
  60.1 26.1 %scatter_custom_fusion = f32[512,256]{1,0:T(8,128)} fusion(s32[4096]{0:T(1024)S(1)} %bitcast.56, f32[4096]{0:T(1024)S(1)} %add_select_fusion, f32[]{:T(128)} %constant.11.clone.1, bf16[4096,256]{1,0:T(8,128)(2,1)S(1)} %gather_fusion, pred[4096]{0:T(1024)(128)(4,1)S(1)} %compare_and_fusion), kind=kCustom, calls=%fused_computation.35 | custom fusion | flops 4194304 | bytes 2641924 | tf_op jit(solution)/shard_map/scatter-add | solution.py:42
  87.4 84.7 %all-reduce.12.cloned.1.call-done = f32[512,256]{1,0:T(8,128)} async-done(((f32[512,256]{1,0:T(8,128)}), f32[512,256]{1,0:T(8,128)}) %all-reduce.12.cloned.1.call-update) | async-done | bytes 524304 | tf_op jit(solution)/shard_map/psum | solution.py:51
  172.1 17.1 %gather_fusion.1 = f32[4096,256]{1,0:T(8,128)} fusion(f32[512,256]{1,0:T(8,128)} %all-reduce.12.cloned.1.call-done, s32[4096]{0:T(1024)S(1)} %broadcast_clamp_fusion), kind=kCustom, calls=%fused_computation.1 | custom fusion | bytes 8404992 | tf_op jit(solution)/shard_map/gather | solution.py:45
  189.2 3.0 fusion.1
  192.2 26.1 %scatter_custom_fusion.1 = f32[512,256]{1,0:T(8,128)} fusion(s32[4096]{0:T(1024)S(1)} %bitcast.57, f32[4096]{0:T(1024)S(1)} %fusion.60, f32[]{:T(128)} %constant.11.clone.1, bf16[4096,256]{1,0:T(8,128)(2,1)S(1)} %gather_fusion, pred[4096]{0:T(1024)(128)(4,1)S(1)} %compare_and_fusion), kind=kCustom, calls=%fused_computation.37 | custom fusion | flops 4194304 | bytes 2641924 | tf_op jit(solution)/shard_map/scatter-add | solution.py:46
  218.3 15.8 %all-reduce.14.cloned.1.call-done = f32[256,256]{1,0:T(8,128)} async-done(((f32[256,256]{1,0:T(8,128)}), f32[256,256]{1,0:T(8,128)}) %all-reduce.14.cloned.1.call-update) | async-done | bytes 262160 | tf_op jit(solution)/shard_map/psum | solution.py:33
  234.5 88.6 %all-reduce.30.cloned.1.call-done = (f32[512,256]{1,0:T(8,128)}, f32[256,256]{1,0:T(8,128)}) async-done(((f32[512,256]{1,0:T(8,128)}, f32[256,256]{1,0:T(8,128)}), (f32[512,256]{1,0:T(8,128)}, f32[256,256]{1,0:T(8,128)})) %all-reduce.30.cloned.1.call-update) | async-done | bytes 786448 | tf_op jit(solution)/shard_map/psum | solution.py:54
  323.1 1.8 multiply_reduce_fusion.14
  326.0 16.1 %gather_fusion.2 = f32[4096,256]{1,0:T(8,128)} fusion(f32[512,256]{1,0:T(8,128)S(1)} %multiply_add_fusion.7, s32[4096]{0:T(1024)S(1)} %broadcast_clamp_fusion), kind=kCustom, calls=%fused_computation.2 | custom fusion | bytes 8404992 | tf_op jit(solution)/shard_map/gather | solution.py:45
  342.1 3.0 fusion.3
  345.1 26.1 %scatter_custom_fusion.2 = f32[512,256]{1,0:T(8,128)} fusion(s32[4096]{0:T(1024)S(1)} %bitcast.58, f32[4096]{0:T(1024)S(1)} %fusion.59, f32[]{:T(128)} %constant.11.clone.1, bf16[4096,256]{1,0:T(8,128)(2,1)S(1)} %gather_fusion, pred[4096]{0:T(1024)(128)(4,1)S(1)} %compare_and_fusion), kind=kCustom, calls=%fused_computation.39 | custom fusion | flops 4194304 | bytes 2641924 | tf_op jit(solution)/shard_map/scatter-add | solution.py:46
  371.2 85.2 %all-reduce.16.cloned.1.call-done = f32[512,256]{1,0:T(8,128)} async-done(((f32[512,256]{1,0:T(8,128)}), f32[512,256]{1,0:T(8,128)}) %all-reduce.16.cloned.1.call-update) | async-done | bytes 524304 | tf_op jit(solution)/shard_map/psum | solution.py:54
  456.5 1.7 multiply_reduce_fusion.12
  458.2 2.1 multiply_reduce_fusion.11
  460.4 16.1 %gather_fusion.3 = f32[4096,256]{1,0:T(8,128)} fusion(f32[512,256]{1,0:T(8,128)S(1)} %multiply_add_fusion.5, s32[4096]{0:T(1024)S(1)} %broadcast_clamp_fusion), kind=kCustom, calls=%fused_computation.3 | custom fusion | bytes 8404992 | tf_op jit(solution)/shard_map/gather | solution.py:45
  476.5 3.5 fusion.5
  480.0 26.5 %scatter_custom_fusion.3 = f32[512,256]{1,0:T(8,128)} fusion(s32[4096]{0:T(1024)S(1)} %bitcast.59, f32[4096]{0:T(1024)S(1)} %fusion.58, f32[]{:T(128)} %constant.11.clone.1, bf16[4096,256]{1,0:T(8,128)(2,1)} %copy-done.1, pred[4096]{0:T(1024)(128)(4,1)S(1)} %compare_and_fusion), kind=kCustom, calls=%fused_computation.41 | custom fusion | flops 4194304 | bytes 2641924 | tf_op jit(solution)/shard_map/scatter-add | solution.py:46
  507.1 84.8 %all-reduce.18.cloned.1.call-done = f32[512,256]{1,0:T(8,128)} async-done(((f32[512,256]{1,0:T(8,128)}), f32[512,256]{1,0:T(8,128)}) %all-reduce.18.cloned.1.call-update) | async-done | bytes 524304 | tf_op jit(solution)/shard_map/psum | solution.py:54
  591.8 1.7 multiply_reduce_fusion.10
  594.9 16.1 %gather_fusion.4 = f32[4096,256]{1,0:T(8,128)} fusion(f32[512,256]{1,0:T(8,128)S(1)} %get-tuple-element.20, s32[4096]{0:T(1024)S(1)} %broadcast_clamp_fusion), kind=kCustom, calls=%fused_computation.4 | custom fusion | bytes 8404992 | tf_op jit(solution)/shard_map/gather | solution.py:45
  610.9 3.0 fusion.7
  614.0 26.1 %scatter_custom_fusion.4 = f32[512,256]{1,0:T(8,128)} fusion(s32[4096]{0:T(1024)S(1)} %bitcast.60, f32[4096]{0:T(1024)S(1)} %fusion.57, f32[]{:T(128)} %constant.11.clone.1, bf16[4096,256]{1,0:T(8,128)(2,1)S(1)} %copy-done.2, pred[4096]{0:T(1024)(128)(4,1)S(1)} %compare_and_fusion), kind=kCustom, calls=%fused_computation.43 | custom fusion | flops 4194304 | bytes 2641924 | tf_op jit(solution)/shard_map/scatter-add | solution.py:46
  640.1 85.2 %all-reduce.20.cloned.1.call-done = f32[512,256]{1,0:T(8,128)} async-done(((f32[512,256]{1,0:T(8,128)}), f32[512,256]{1,0:T(8,128)}) %all-reduce.20.cloned.1.call-update) | async-done | bytes 524304 | tf_op jit(solution)/shard_map/psum | solution.py:54
  725.4 1.7 multiply_reduce_fusion.8
  728.3 16.1 %gather_fusion.5 = f32[4096,256]{1,0:T(8,128)} fusion(f32[512,256]{1,0:T(8,128)S(1)} %multiply_add_fusion.3, s32[4096]{0:T(1024)S(1)} %broadcast_clamp_fusion), kind=kCustom, calls=%fused_computation.5 | custom fusion | bytes 8404992 | tf_op jit(solution)/shard_map/gather | solution.py:45
  744.4 2.9 fusion.9
  747.3 26.1 %scatter_custom_fusion.5 = f32[512,256]{1,0:T(8,128)} fusion(s32[4096]{0:T(1024)S(1)} %bitcast.61, f32[4096]{0:T(1024)S(1)} %fusion.56, f32[]{:T(128)} %constant.11.clone.1, bf16[4096,256]{1,0:T(8,128)(2,1)S(1)} %copy-done.2, pred[4096]{0:T(1024)(128)(4,1)S(1)} %compare_and_fusion), kind=kCustom, calls=%fused_computation.45 | custom fusion | flops 4194304 | bytes 2641924 | tf_op jit(solution)/shard_map/scatter-add | solution.py:46
  773.7 85.1 %all-reduce.22.cloned.1.call-done = f32[512,256]{1,0:T(8,128)} async-done(((f32[512,256]{1,0:T(8,128)}), f32[512,256]{1,0:T(8,128)}) %all-reduce.22.cloned.1.call-update) | async-done | bytes 524304 | tf_op jit(solution)/shard_map/psum | solution.py:54
  858.8 1.7 multiply_reduce_fusion.6
  860.5 1.3 multiply_reduce_fusion.5
  862.0 16.1 %gather_fusion.6 = f32[4096,256]{1,0:T(8,128)} fusion(f32[512,256]{1,0:T(8,128)S(1)} %multiply_add_fusion.2, s32[4096]{0:T(1024)S(1)} %broadcast_clamp_fusion), kind=kCustom, calls=%fused_computation.6 | custom fusion | bytes 8404992 | tf_op jit(solution)/shard_map/gather | solution.py:45
  878.0 3.5 fusion.11
  881.5 26.5 %scatter_custom_fusion.6 = f32[512,256]{1,0:T(8,128)} fusion(s32[4096]{0:T(1024)S(1)} %bitcast.62, f32[4096]{0:T(1024)S(1)} %fusion.55, f32[]{:T(128)} %constant.11.clone.1, bf16[4096,256]{1,0:T(8,128)(2,1)} %copy-done.1, pred[4096]{0:T(1024)(128)(4,1)S(1)} %compare_and_fusion), kind=kCustom, calls=%fused_computation.47 | custom fusion | flops 4194304 | bytes 2641924 | tf_op jit(solution)/shard_map/scatter-add | solution.py:46
  908.1 85.2 %all-reduce.24.cloned.1.call-done = f32[512,256]{1,0:T(8,128)} async-done(((f32[512,256]{1,0:T(8,128)}), f32[512,256]{1,0:T(8,128)}) %all-reduce.24.cloned.1.call-update) | async-done | bytes 524304 | tf_op jit(solution)/shard_map/psum | solution.py:54
  993.4 1.7 multiply_reduce_fusion.4
  995.5 16.1 %gather_fusion.7 = f32[4096,256]{1,0:T(8,128)} fusion(f32[512,256]{1,0:T(8,128)S(1)} %multiply_add_fusion.1, s32[4096]{0:T(1024)S(1)} %broadcast_clamp_fusion), kind=kCustom, calls=%fused_computation.7 | custom fusion | bytes 8404992 | tf_op jit(solution)/shard_map/gather | solution.py:45
  1011.6 3.5 fusion.13
  1015.0 26.5 %scatter_custom_fusion.7 = f32[512,256]{1,0:T(8,128)} fusion(s32[4096]{0:T(1024)S(1)} %bitcast.63, f32[4096]{0:T(1024)S(1)} %fusion.54, f32[]{:T(128)} %constant.11.clone.1, bf16[4096,256]{1,0:T(8,128)(2,1)} %copy-done.1, pred[4096]{0:T(1024)(128)(4,1)S(1)} %compare_and_fusion), kind=kCustom, calls=%fused_computation.49 | custom fusion | flops 4194304 | bytes 2641924 | tf_op jit(solution)/shard_map/scatter-add | solution.py:46
  1041.8 85.0 %all-reduce.26.cloned.1.call-done = f32[512,256]{1,0:T(8,128)} async-done(((f32[512,256]{1,0:T(8,128)}), f32[512,256]{1,0:T(8,128)}) %all-reduce.26.cloned.1.call-update) | async-done | bytes 524304 | tf_op jit(solution)/shard_map/psum | solution.py:54
  1126.8 1.7 multiply_reduce_fusion.2
  1128.9 16.1 %gather_fusion.8 = f32[4096,256]{1,0:T(8,128)} fusion(f32[512,256]{1,0:T(8,128)S(1)} %multiply_add_fusion, s32[4096]{0:T(1024)S(1)} %broadcast_clamp_fusion), kind=kCustom, calls=%fused_computation.8 | custom fusion | bytes 8404992 | tf_op jit(solution)/shard_map/gather | solution.py:45
  1145.0 3.5 fusion.15
  1148.5 26.5 %scatter_custom_fusion.8 = f32[512,256]{1,0:T(8,128)} fusion(s32[4096]{0:T(1024)S(1)} %bitcast.64, f32[4096]{0:T(1024)S(1)} %fusion.53, f32[]{:T(128)} %constant.11.clone.1, bf16[4096,256]{1,0:T(8,128)(2,1)} %copy-done.1, pred[4096]{0:T(1024)(128)(4,1)S(1)} %compare_and_fusion), kind=kCustom, calls=%fused_computation.51 | custom fusion | flops 4194304 | bytes 2641924 | tf_op jit(solution)/shard_map/scatter-add | solution.py:46
  1175.3 85.0 %all-reduce.28.cloned.1.call-done = f32[512,256]{1,0:T(8,128)} async-done(((f32[512,256]{1,0:T(8,128)}), f32[512,256]{1,0:T(8,128)}) %all-reduce.28.cloned.1.call-update) | async-done | bytes 524304 | tf_op jit(solution)/shard_map/psum | solution.py:54
  1260.3 1.7 multiply_reduce_fusion
  1262.1 1.5 fusion.45
  (91 shorter events, 10.8 us)
Async XLA Ops:
  7.2 37.1 %all-gather.3.cloned.1.call-start = ((), (), s32[]{:S(2)}) async-start(), calls=%async_computation.9 | async-start | bytes 4718592 | tf_op jit(solution)/shard_map/all_gather | solution.py:30
  7.9 164.2 %all-reduce.12.cloned.1.call-start = ((), (), s32[]{:S(2)}) async-start(), calls=%async_computation | async-start | bytes 1048576 | tf_op jit(solution)/shard_map/psum | solution.py:51
  44.3 15.8 %copy-start.10 = (s32[1,1,4096]{2,1,0:T(1,128)S(1)}, s32[1,1,4096]{2,1,0:T(1,128)}, u32[]{:S(2)}) copy-start(s32[1,1,4096]{2,1,0:T(1,128)} %param.7) | copy-start | bytes 49156
  44.3 42.0 %copy-start.9 = (bf16[1,1024,256]{2,1,0:T(8,128)(2,1)S(1)}, bf16[1,1024,256]{2,1,0:T(8,128)(2,1)}, u32[]{:S(2)}) copy-start(bf16[1,1024,256]{2,1,0:T(8,128)(2,1)} %param.5) | copy-start | bytes 1572868
  60.1 285.0 %copy-start.1 = (bf16[4096,256]{1,0:T(8,128)(2,1)}, bf16[4096,256]{1,0:T(8,128)(2,1)S(1)}, u32[]{:S(2)}) copy-start(bf16[4096,256]{1,0:T(8,128)(2,1)S(1)} %gather_fusion) | copy-start | bytes 6291460
  86.2 148.0 %all-reduce.14.cloned.1.call-start = ((), (), s32[]{:S(2)}) async-start(), calls=%async_computation.1 | async-start | bytes 524288 | tf_op jit(solution)/shard_map/psum | solution.py:33
  87.3 235.8 %all-reduce.30.cloned.1.call-start = ((), (), s32[]{:S(2)}) async-start(), calls=%async_computation.10 | async-start | bytes 1572864 | tf_op jit(solution)/shard_map/psum | solution.py:54
  189.2 3.0 copy-start.8
  189.2 133.9 %copy-start = (f32[512,256]{1,0:T(8,128)S(1)}, f32[512,256]{1,0:T(8,128)}, u32[]{:S(2)}) copy-start(f32[512,256]{1,0:T(8,128)} %all-reduce.12.cloned.1.call-done) | copy-start | bytes 1572868
  234.2 222.3 %all-reduce.16.cloned.1.call-start = ((), (), s32[]{:S(2)}) async-start(), calls=%async_computation.2 | async-start | bytes 1048576 | tf_op jit(solution)/shard_map/psum | solution.py:54
  324.9 0.8 copy-start.4
  342.1 114.4 %copy-start.3 = (f32[256,256]{1,0:T(8,128)S(1)}, f32[256,256]{1,0:T(8,128)}, u32[]{:S(2)}) copy-start(f32[256,256]{1,0:T(8,128)} %get-tuple-element.5) | copy-start | bytes 786436
  371.2 220.6 %all-reduce.18.cloned.1.call-start = ((), (), s32[]{:S(2)}) async-start(), calls=%async_computation.3 | async-start | bytes 1048576 | tf_op jit(solution)/shard_map/psum | solution.py:54
  506.5 218.9 %all-reduce.20.cloned.1.call-start = ((), (), s32[]{:S(2)}) async-start(), calls=%async_computation.4 | async-start | bytes 1048576 | tf_op jit(solution)/shard_map/psum | solution.py:54
  593.8 1.0 copy-start.6
  594.9 16.1 %copy-start.2 = (bf16[4096,256]{1,0:T(8,128)(2,1)S(1)}, bf16[4096,256]{1,0:T(8,128)(2,1)}, u32[]{:S(2)}) copy-start(bf16[4096,256]{1,0:T(8,128)(2,1)} %copy-done.1) | copy-start | bytes 6291460
  610.9 116.2 %copy-start.7 = (f32[512,256]{1,0:T(8,128)S(1)}, f32[512,256]{1,0:T(8,128)}, u32[]{:S(2)}) copy-start(f32[512,256]{1,0:T(8,128)} %copy-done.6) | copy-start | bytes 1572868
  640.1 218.7 %all-reduce.22.cloned.1.call-start = ((), (), s32[]{:S(2)}) async-start(), calls=%async_computation.5 | async-start | bytes 1048576 | tf_op jit(solution)/shard_map/psum | solution.py:54
  727.3 0.8 copy-start.5
  773.5 219.9 %all-reduce.24.cloned.1.call-start = ((), (), s32[]{:S(2)}) async-start(), calls=%async_computation.6 | async-start | bytes 1048576 | tf_op jit(solution)/shard_map/psum | solution.py:54
  908.1 218.7 %all-reduce.26.cloned.1.call-start = ((), (), s32[]{:S(2)}) async-start(), calls=%async_computation.7 | async-start | bytes 1048576 | tf_op jit(solution)/shard_map/psum | solution.py:54
  1041.6 218.7 %all-reduce.28.cloned.1.call-start = ((), (), s32[]{:S(2)}) async-start(), calls=%async_computation.8 | async-start | bytes 1048576 | tf_op jit(solution)/shard_map/psum | solution.py:54
Sparse Core Ops, SparseCore 0:
  9.7 34.5 all-gather.2
  86.3 85.7 all-reduce.11
  174.4 59.7 all-reduce.13
  237.4 85.7 all-reduce.29
  371.3 85.0 all-reduce.15
  506.6 85.1 all-reduce.17
  640.2 85.1 all-reduce.19
  773.6 85.1 all-reduce.21
  908.2 85.1 all-reduce.23
  1041.7 85.0 all-reduce.25
  1175.1 85.1 all-reduce.27
